TPU v7x, 32 devices: a whole 2x2x4 slice. The times are simulated.
32 devices in a mesh: dp: 8 (over y, x, core), seq: 4 (over z).
Axes of the slice: x: 2, y: 2, z: 4, core: 2. Of those that a mesh axis runs over, the one named last changes fastest.
Arguments:
- tokens: bfloat16 [8, 8, 64, 3072], P('dp', 'seq'), may hold values from -6 to 6
- frozen_projection: bfloat16 [8, 8, 64, 4608], P('dp', 'seq'), may hold values from -6 to 6
- output_gradient: bfloat16 [8, 8, 64, 1536], P('dp', 'seq'), may hold values from -6 to 6
- adapter_down: bfloat16 [3072, 8], replicated, may hold values from -0.109375 to 0.109375
- adapter_up: bfloat16 [8, 4608], replicated, may hold values from -2 to 2
- query_norm_gain: float32 [128], replicated, may hold values from 0.5 to 1.5
- key_norm_gain: float32 [128], replicated, may hold values from 0.5 to 1.5
- neighbour_mask: int32 [4, 12, 2], replicated, may hold values 0 or 1
Outputs:
- grad_qkv: bfloat16 [8, 8, 64, 4608], P('dp', 'seq')
- lora_down_grad: float32 [3072, 8], P('dp')
- lora_up_grad: float32 [8, 4608], P(None, 'dp')
All inputs are finite; a program needn't handle non-finite values.
Results may differ from a plain program's by a relative error of at most 0.0072.
Values may be sent and summed in bfloat16 or wider, within the bound.
A program may use at most 64 MiB of HBM per device.

v0:
```python
import jax
import jax.numpy as jnp
from jax import lax
from jax.sharding import PartitionSpec as P

epsilon = 1e-06


def shifted(x, axis, by):
    size = lax.axis_size(axis)
    pairs = [(i, i + by) for i in range(size) if 0 <= i + by < size]
    return lax.ppermute(x, axis, pairs)


def head_norm(values, gain_vector):
    inverse = lax.rsqrt(jnp.mean(values * values, axis=-1, keepdims=True) + epsilon)
    return (values * inverse * gain_vector, inverse)


def head_norm_grad(values, inverse, gain_vector, upstream):
    scaled = upstream * gain_vector
    return inverse * scaled - values * inverse * inverse * inverse * jnp.mean(
        scaled * values, axis=-1, keepdims=True
    )


def to_heads(rows, head_count):
    clip_count, row_count, width = rows.shape
    return rows.reshape(clip_count, row_count, head_count, width // head_count).transpose(
        0, 2, 1, 3
    )


def from_heads(heads):
    clip_count, head_count, row_count, head_dim = heads.shape
    return heads.transpose(0, 2, 1, 3).reshape(clip_count, row_count, head_count * head_dim)


def fetch_keys(key_value, distance):
    return shifted(key_value, "seq", distance)


def return_piece(piece, distance):
    return shifted(piece, "seq", distance)


def attend(queries, upstream, key_bank, value_bank, allowed):
    head_dim = queries.shape[-1]
    score_scale = head_dim ** (-0.5)
    scores = (
        jnp.einsum("hqd,hkd->hqk", queries, key_bank, preferred_element_type=jnp.float32)
        * score_scale
    )
    raw_weights = jnp.exp(scores) * allowed[:, None, :]
    totals = jnp.sum(raw_weights, axis=-1, keepdims=True)
    weights = raw_weights / totals
    weights_low = weights.astype(jnp.bfloat16)
    grad_weights = jnp.einsum(
        "hqd,hkd->hqk", upstream, value_bank, preferred_element_type=jnp.float32
    )
    row_delta = jnp.sum(weights * grad_weights, axis=-1, keepdims=True)
    grad_scores = (weights * (grad_weights - row_delta)).astype(jnp.bfloat16)
    grad_queries = (
        jnp.einsum("hqk,hkd->hqd", grad_scores, key_bank, preferred_element_type=jnp.float32)
        * score_scale
    )
    grad_keys = (
        jnp.einsum("hqk,hqd->hkd", grad_scores, queries, preferred_element_type=jnp.float32)
        * score_scale
    ).astype(jnp.bfloat16)
    grad_values = jnp.einsum(
        "hqk,hqd->hkd", weights_low, upstream, preferred_element_type=jnp.float32
    ).astype(jnp.bfloat16)
    return (grad_queries, grad_keys, grad_values, totals[..., 0], row_delta[..., 0])


def on_device(
    tokens,
    frozen_projection,
    output_gradient,
    adapter_down,
    adapter_up,
    query_norm_gain,
    key_norm_gain,
    neighbour_mask,
):
    clip_count, frames_dev, spatial, model_width = tokens.shape
    combined_width = frozen_projection.shape[-1]
    embed_width = combined_width // 3
    head_dim = query_norm_gain.shape[0]
    head_count = embed_width // head_dim
    query_rows = frames_dev * spatial
    seq_devices = lax.axis_size("seq")
    frame_count = frames_dev * seq_devices
    head_shape = (clip_count, frames_dev, spatial, head_count, head_dim)
    slab_shape = (clip_count, frames_dev, spatial, embed_width)
    token_matrix = tokens.reshape(-1, model_width)
    reduced_rows = jnp.dot(token_matrix, adapter_down, preferred_element_type=jnp.float32).astype(
        jnp.bfloat16
    )
    projected_rows = frozen_projection.reshape(-1, combined_width).astype(jnp.float32) + jnp.dot(
        reduced_rows, adapter_up, preferred_element_type=jnp.float32
    )
    query_raw = projected_rows[:, :embed_width].reshape(head_shape)
    key_raw = projected_rows[:, embed_width : 2 * embed_width].reshape(head_shape)
    query_normed, query_inverse = head_norm(query_raw, query_norm_gain)
    key_normed, key_inverse = head_norm(key_raw, key_norm_gain)
    query_low = query_normed.astype(jnp.bfloat16).reshape(clip_count, query_rows, embed_width)
    key_low = key_normed.astype(jnp.bfloat16).reshape(clip_count, query_rows, embed_width)
    value_low = (
        projected_rows[:, 2 * embed_width :]
        .astype(jnp.bfloat16)
        .reshape(clip_count, query_rows, embed_width)
    )
    upstream_rows = output_gradient.reshape(clip_count, query_rows, embed_width)
    key_value = jnp.concatenate([key_low, value_low], axis=-1)
    seq_index = lax.axis_index("seq")
    keep_row = lax.dynamic_index_in_dim(neighbour_mask, seq_index, 0, keepdims=False).astype(
        jnp.float32
    )
    has_below = (seq_index > 0).astype(jnp.float32)
    has_above = (seq_index < seq_devices - 1).astype(jnp.float32)
    below_kv = fetch_keys(key_value, 1)
    above_kv = fetch_keys(key_value, -1)
    bank = jnp.concatenate([below_kv, key_value, above_kv], axis=1)
    key_bank = to_heads(bank[..., :embed_width], head_count)
    value_bank = to_heads(bank[..., embed_width:], head_count)
    queries = to_heads(query_low, head_count)
    upstream = to_heads(upstream_rows, head_count)
    slot_allow = jnp.stack(
        [
            keep_row[:, 0] * has_below,
            jnp.ones((head_count,), jnp.float32),
            keep_row[:, 1] * has_above,
        ],
        axis=1,
    )
    allowed = jnp.broadcast_to(slot_allow[:, :, None], (head_count, 3, query_rows)).reshape(
        head_count, 3 * query_rows
    )
    grad_queries, grad_keys, grad_values, totals, deltas = jax.vmap(
        attend, in_axes=(0, 0, 0, 0, None)
    )(queries, upstream, key_bank, value_bank, allowed)
    grad_queries = from_heads(grad_queries).reshape(head_shape)
    bank_grad = jnp.concatenate([from_heads(grad_keys), from_heads(grad_values)], axis=-1)
    summed = lax.slice_in_dim(bank_grad, query_rows, 2 * query_rows, axis=1).astype(jnp.float32)
    for position in (-1, 1):
        slot_first = (position + 1) * query_rows
        slot_piece = lax.slice_in_dim(bank_grad, slot_first, slot_first + query_rows, axis=1)
        summed = summed + return_piece(slot_piece, position).astype(jnp.float32)
    grad_key_sum = summed[..., :embed_width].reshape(head_shape)
    grad_value_sum = summed[..., embed_width:].reshape(slab_shape)
    grad_query_raw = head_norm_grad(query_raw, query_inverse, query_norm_gain, grad_queries)
    grad_key_raw = head_norm_grad(key_raw, key_inverse, key_norm_gain, grad_key_sum)
    grad_qkv = jnp.concatenate(
        [grad_query_raw.reshape(slab_shape), grad_key_raw.reshape(slab_shape), grad_value_sum],
        axis=-1,
    ).astype(jnp.bfloat16)
    gradient_rows = grad_qkv.reshape(-1, combined_width)
    gradient_reduced = lax.dot_general(
        gradient_rows, adapter_up, (((1,), (1,)), ((), ())), preferred_element_type=jnp.float32
    ).astype(jnp.bfloat16)
    term_up = lax.dot_general(
        reduced_rows, gradient_rows, (((0,), (0,)), ((), ())), preferred_element_type=jnp.float32
    )
    term_down = lax.dot_general(
        token_matrix, gradient_reduced, (((0,), (0,)), ((), ())), preferred_element_type=jnp.float32
    )
    dp_devices = lax.axis_size("dp")
    norm_factor = float(clip_count * dp_devices * frame_count * spatial) ** (-0.5)
    whole_down, whole_up = lax.psum((term_down, term_up), ("dp", "seq"))
    dp_index = lax.axis_index("dp")
    row_share = model_width // dp_devices
    column_share = combined_width // dp_devices
    grad_down = lax.dynamic_slice_in_dim(whole_down, dp_index * row_share, row_share, 0)
    grad_up = lax.dynamic_slice_in_dim(whole_up, dp_index * column_share, column_share, 1)
    return (grad_qkv, grad_down * norm_factor, grad_up * norm_factor)


def solution(mesh):
    return jax.shard_map(
        on_device,
        mesh=mesh,
        in_specs=(
            P("dp", "seq", None, None),
            P("dp", "seq", None, None),
            P("dp", "seq", None, None),
            P(),
            P(),
            P(),
            P(),
            P(),
        ),
        out_specs=(P("dp", "seq", None, None), P("dp", None), P(None, "dp")),
        check_vma=False,
    )
```

profile of v0, /device:TPU:0, one launch (start us, length us, event | category | flops | bytes accessed | tf_op | source)
XLA Modules:
  0.0 263.6 jit_solution(1153756747695286428)
XLA Ops:
  7.2 1.1 copy-done
  8.3 1.1 convolution_convert_fusion.2
  9.4 1.8 convolution_add_fusion
  11.3 0.9 slice.50
  12.2 0.8 fusion.30
  13.0 2.2 reshape.418
  15.3 1.6 multiply_reduce_fusion.1
  17.2 1.3 fusion.40
  18.5 1.0 pad_maximum_fusion.4
  19.5 5.8 %collective-permute-start = (bf16[1,128,3072]{2,1,0:T(8,128)(2,1)}, bf16[1,128,3072]{2,1,0:T(8,128)(2,1)}, u32[]{:S(2)}, u32[]{:S(2)}) collective-permute-start(bf16[1,128,3072]{2,1,0:T(8,128)(2,1)} %pad_maximum_fusion.4), channel_id=1, source_target_pairs={{0,1},{1,2},{2,3},{4,5},{5,6},{6,7},{8,9},{9,10},{10,11},{12,13},{... | collective-permute-start | bytes 2359304 | tf_op jit(solution)/shard_map/ppermute | solution.py:12
  25.3 1.3 collective-permute-start.1
  26.6 2.3 reshape.415
  28.9 2.3 copy.24
  31.2 0.7 convert_bitcast_fusion
  32.6 0.8 copy.29
  34.1 1.6 multiply_reduce_fusion.2
  36.3 0.9 copy.43
  37.2 2.2 reshape_reshape.11
  39.3 2.1 copy.36
  41.6 5.0 %collective-permute-done.1 = bf16[1,128,3072]{2,1,0:T(8,128)(2,1)} collective-permute-done((bf16[1,128,3072]{2,1,0:T(8,128)(2,1)}, bf16[1,128,3072]{2,1,0:T(8,128)(2,1)}, u32[]{:S(2)}, u32[]{:S(2)}) %collective-permute-start.1) | collective-permute-done | bytes 786464 | tf_op jit(solution)/shard_map/ppermute | solution.py:12
  46.6 1.7 pad_maximum_fusion
  48.2 1.6 fusion.39
  49.9 2.4 copy.26
  52.2 2.4 copy.27
  54.6 2.4 copy.30
  57.0 2.4 copy.31
  59.4 2.3 fusion.4
  61.8 1.8 convolution_convert_fusion
  64.0 2.3 fusion
  66.3 2.4 copy.38
  68.7 2.8 %fusion.2 = bf16[12,128,384]{2,1,0:T(8,128)(2,1)S(1)} fusion(f32[12,384,128]{1,2,0:T(8,128)} %get-tuple-element.18, f32[12,128]{1,0:T(8,128)S(1)} %get-tuple-element.17, f32[12,128]{1,0:T(8,128)S(1)} %get-tuple-element.15, f32[12,384]{1,0:T(8,128)S(1)} %bitcast.158, f32[12,128,384]{2,1,0:T(8,128)} %copy-done.7), kind=kLoop, calls=%fused_computation.11 | loop fusion | flops 3538944 | bytes 5928960 | tf_op jit(solution)/shard_map/vmap()/convert_element_type | solution.py:62
  71.5 1.0 copy-done.4
  72.5 1.5 multiply_convert_fusion
  74.0 2.4 copy.37
  76.4 2.7 %fusion.25 = (bf16[1,128,3072]{2,1,0:T(8,128)(2,1)}, bf16[1,128,3072]{2,1,0:T(8,128)(2,1)}) fusion(bf16[1,384,1536]{2,1,0:T(8,128)(2,1)} %copy.37, bf16[1,384,1536]{2,1,0:T(8,128)(2,1)} %copy.38), kind=kLoop, calls=%fused_computation.51 | loop fusion | flops 3145728 | bytes 3932160 | tf_op jit(solution)/shard_map/concatenate | solution.py:145
  79.2 1.3 collective-permute-start.2
  80.4 5.4 %collective-permute-start.3 = (bf16[1,128,3072]{2,1,0:T(8,128)(2,1)}, bf16[1,128,3072]{2,1,0:T(8,128)(2,1)}, u32[]{:S(2)}, u32[]{:S(2)}) collective-permute-start(bf16[1,128,3072]{2,1,0:T(8,128)(2,1)} %get-tuple-element.8), channel_id=1, source_target_pairs={{0,1},{1,2},{2,3},{4,5},{5,6},{6,7},{8,9},{9,10},{10,11},{12,13},{... | collective-permute-start | bytes 2359304 | tf_op jit(solution)/shard_map/ppermute | solution.py:12
  85.9 2.2 mul.501
  88.1 1.3 mul.459
  89.5 2.2 mul.460
  91.7 3.0 %convolution_multiply_fusion = f32[12,128,128]{2,1,0:T(8,128)} fusion(bf16[12,128,384]{2,1,0:T(8,128)(2,1)} %copy-done.4, bf16[1,384,12,128]{3,1,2,0:T(8,128)(2,1)} %copy.27), kind=kOutput, calls=%fused_computation.18 | convolution fusion | flops 151191552 | bytes 3145728 | tf_op jit(solution)/shard_map/vmap(hqk,hkd->hqd)/dot_general | solution.py:64
  94.7 2.3 copy.39
  97.0 2.6 copy.34
  99.6 2.3 copy.40
  101.9 2.0 fusion.12
  103.9 1.4 mul.498
  105.3 2.2 mul.499
  107.5 2.3 reshape_reshape.12
  109.8 1.9 convert_add_fusion
  111.7 1.1 slice.58
  113.1 0.8 slice_bitcast_fusion
  113.9 2.2 reshape.430
  116.2 2.0 multiply_reduce_fusion
  118.7 3.3 %fusion.21 = (bf16[128,1536]{1,0:T(8,128)(2,1)S(1)}, bf16[128,1536]{1,0:T(8,128)(2,1)S(1)}) fusion(f32[16,8,12,128]{3,2,1,0:T(8,128)} %bitcast.140, f32[16,8,12,128]{3,2,1,0:T(8,128)} %bitcast.139, f32[128,1536]{1,0:T(8,128)S(1)} %copy-done.12, f32[1536]{0:T(1024)S(1)} %broadcast_bitcast_fusion, f32[128,4608]{1,0:T(8,128)S(1)} %convolution_add_fusion, ...), kind=kLoop, calls=%fused_computation.47 | loop fusion | flops 3145728 | bytes 7090176 | tf_op jit(solution)/shard_map/convert.1
  122.1 0.7 copy-done.15
  122.8 0.9 fusion.27
  123.8 2.6 convolution_bitcast_fusion
  126.3 1.0 mul.514
  127.3 1.2 slice.84
  128.6 3.3 %fusion.31 = (bf16[1,2,64,1536]{3,2,1,0:T(8,128)(2,1)S(1)}, bf16[1,2,64,1536]{3,2,1,0:T(8,128)(2,1)S(1)}) fusion(f32[2,64,1536]{2,1,0:T(8,128)} %mul.514, f32[2,64,1536]{2,1,0:T(8,128)} %mul.501, f32[2,64,1536]{2,1,0:T(8,128)} %bitcast.142, f32[2,64,1536]{2,1,0:T(8,128)} %bitcast.143, f32[1536]{0:T(1024)S(1)} %broadcast_bitcast_fusion.1, ...), kind=kLoop, calls=%fused_computation.67 | loop fusion | flops 3145728 | bytes 7090176 | tf_op jit(solution)/shard_map/concatenate | solution.py:155
  131.9 1.1 pad_maximum_fusion.1
  132.9 121.1 %all-reduce.3.cloned.1.call-done = (f32[3072,8]{0,1:T(8,128)}, f32[8,4608]{1,0:T(8,128)}) async-done(((f32[3072,8]{0,1:T(8,128)}, f32[8,4608]{1,0:T(8,128)}), (f32[3072,8]{0,1:T(8,128)}, f32[8,4608]{1,0:T(8,128)})) %all-reduce.3.cloned.1.call-update) | async-done | bytes 245776 | tf_op jit(solution)/shard_map/psum | solution.py:171
  254.0 1.4 dynamic-slice_multiply_fusion
  255.4 1.3 dynamic-slice_multiply_fusion.1
  (68 shorter events, 3.9 us)
Async XLA Ops:
  7.2 1.1 copy-start
  7.2 246.8 %all-reduce.3.cloned.1.call-start = ((), (), s32[]{:S(2)}) async-start(), calls=%async_computation | async-start | bytes 491520 | tf_op jit(solution)/shard_map/psum | solution.py:171
  9.4 2.8 %copy-start.21 = (bf16[128,8]{0,1:T(8,128)(2,1)}, bf16[128,8]{0,1:T(8,128)(2,1)S(1)}, u32[]{:S(2)}) copy-start(bf16[128,8]{0,1:T(8,128)(2,1)S(1)} %convolution_convert_fusion.2) | copy-start | bytes 6148
  11.3 5.6 %copy-start.24 = (f32[128]{0:T(128)S(1)}, f32[128]{0:T(128)}, u32[]{:S(2)}) copy-start(f32[128]{0:T(128)} %param.14) | copy-start | bytes 1540
  16.9 1.7 copy-start.11
  17.2 2.3 copy-start.1
  19.5 22.1 %collective-permute-start = (bf16[1,128,3072]{2,1,0:T(8,128)(2,1)}, bf16[1,128,3072]{2,1,0:T(8,128)(2,1)}, u32[]{:S(2)}, u32[]{:S(2)}) collective-permute-start(bf16[1,128,3072]{2,1,0:T(8,128)(2,1)} %pad_maximum_fusion.4), channel_id=1, source_target_pairs={{0,1},{1,2},{2,3},{4,5},{5,6},{6,7},{8,9},{9,10},{10,11},{12,13},{... | collective-permute-start | bytes 2359304 | tf_op jit(solution)/shard_map/ppermute | solution.py:12
  25.3 21.2 %collective-permute-start.1 = (bf16[1,128,3072]{2,1,0:T(8,128)(2,1)}, bf16[1,128,3072]{2,1,0:T(8,128)(2,1)}, u32[]{:S(2)}, u32[]{:S(2)}) collective-permute-start(bf16[1,128,3072]{2,1,0:T(8,128)(2,1)} %pad_maximum_fusion.4), channel_id=1, source_target_pairs={{1,0},{2,1},{3,2},{5,4},{6,5},{7,6},{9,8},{10,9},{11,10},{13,12},{... | collective-permute-start | bytes 2359304 | tf_op jit(solution)/shard_map/ppermute | solution.py:12
  54.6 4.8 %copy-start.19 = (f32[2,8,3,128]{3,1,2,0:T(8,128)S(1)}, f32[2,8,3,128]{3,1,2,0:T(8,128)}, u32[]{:S(2)}) copy-start(f32[2,8,3,128]{3,1,2,0:T(8,128)} %copy.45) | copy-start | bytes 73732
  54.6 4.8 %copy-start.23 = (f32[128]{0:T(128)S(1)}, f32[128]{0:T(128)}, u32[]{:S(2)}) copy-start(f32[128]{0:T(128)} %param.13) | copy-start | bytes 1540
  59.4 2.4 copy-start.16
  61.8 1.9 copy-start.7
  61.8 2.2 copy-start.13
  68.7 3.8 %copy-start.10 = (f32[128,1536]{0,1:T(8,128)S(1)}, f32[128,1536]{0,1:T(8,128)}, u32[]{:S(2)}) copy-start(f32[128,1536]{0,1:T(8,128)} %copy.24) | copy-start | bytes 2359300
  71.5 1.0 copy-start.4
  76.4 11.7 %copy-start.14 = (f32[2,64,12]{2,1,0:T(8,128)S(1)}, f32[2,64,12]{2,1,0:T(8,128)}, u32[]{:S(2)}) copy-start(f32[2,64,12]{2,1,0:T(8,128)} %add_rsqrt_fusion.1) | copy-start | bytes 18436
  79.2 30.6 %collective-permute-start.2 = (bf16[1,128,3072]{2,1,0:T(8,128)(2,1)}, bf16[1,128,3072]{2,1,0:T(8,128)(2,1)}, u32[]{:S(2)}, u32[]{:S(2)}) collective-permute-start(bf16[1,128,3072]{2,1,0:T(8,128)(2,1)} %get-tuple-element.7), channel_id=1, source_target_pairs={{1,0},{2,1},{3,2},{5,4},{6,5},{7,6},{9,8},{10,9},{11,10},{13,12},{... | collective-permute-start | bytes 2359304 | tf_op jit(solution)/shard_map/ppermute | solution.py:12
  80.4 29.3 %collective-permute-start.3 = (bf16[1,128,3072]{2,1,0:T(8,128)(2,1)}, bf16[1,128,3072]{2,1,0:T(8,128)(2,1)}, u32[]{:S(2)}, u32[]{:S(2)}) collective-permute-start(bf16[1,128,3072]{2,1,0:T(8,128)(2,1)} %get-tuple-element.8), channel_id=1, source_target_pairs={{0,1},{1,2},{2,3},{4,5},{5,6},{6,7},{8,9},{9,10},{10,11},{12,13},{... | collective-permute-start | bytes 2359304 | tf_op jit(solution)/shard_map/ppermute | solution.py:12
  111.7 1.5 copy-start.5
  111.7 4.5 %copy-start.25 = (f32[128]{0:T(128)S(1)}, f32[128]{0:T(128)}, u32[]{:S(2)}) copy-start(f32[128]{0:T(128)} %param.14) | copy-start | bytes 1540
  116.2 2.4 copy-start.2
  116.2 2.4 copy-start.6
  116.2 2.5 copy-start.12
  118.6 3.5 %copy-start.8 = (f32[2,64,12,128]{3,2,1,0:T(8,128)}, f32[2,64,12,128]{3,2,1,0:T(8,128)S(1)}, u32[]{:S(2)}) copy-start(f32[2,64,12,128]{3,2,1,0:T(8,128)S(1)} %mul.513) | copy-start | bytes 2359300
  118.7 4.1 %copy-start.17 = (bf16[128,1536]{1,0:T(8,128)(2,1)S(1)}, bf16[128,1536]{1,0:T(8,128)(2,1)}, u32[]{:S(2)}) copy-start(bf16[128,1536]{1,0:T(8,128)(2,1)} %slice_bitcast_fusion) | copy-start | bytes 1179652
  118.7 4.1 %copy-start.22 = (bf16[128,8]{0,1:T(8,128)(2,1)S(1)}, bf16[128,8]{0,1:T(8,128)(2,1)}, u32[]{:S(2)}) copy-start(bf16[128,8]{0,1:T(8,128)(2,1)} %copy-done.21) | copy-start | bytes 6148
  122.0 0.8 copy-start.15
  122.1 1.7 copy-start.18
  122.1 1.7 copy-start.20
  123.7 2.6 copy-start.9
  126.3 2.2 copy-start.3
Sparse Core Ops, SparseCore 0:
  128.7 125.3 all-reduce.2
where the time goes:
time: 265 us; the launch traced here: 264 us
  waiting for transfers between devices  126 us (48%)
  local copies, waits for them, and re-layouts  60.8 us (23%)
  other arithmetic  30.9 us (12%)
  matrix products  17.4 us (7%)
  between operations  14.3 us (5%)
  starting transfers between devices  13.9 us (5%)
    psum x1, waiting for transfers between devices, on_device(): whole_down, whole_up = lax.psum((term_down, term_up), ('dp', 'seq'))  121 us
    ppermute x4, starting transfers between devices, shifted(): return lax.ppermute(x, axis, pairs)  13.8 us
  transfers between devices with their start and end apart: 5, of which 3 were waited for; matrix products, arithmetic and copies ran while one was open for 16% of the time, Pallas kernels for 0%

commit v1 on v0

v1 whole, which is shorter than its diff:
```python
import functools

import jax
import jax.numpy as jnp
from jax import lax
from jax.experimental import pallas as pl
from jax.experimental.pallas import tpu as pltpu
from jax.sharding import PartitionSpec as P

EPSILON = 1e-06
CHUNKS = (2, 2, 2, 2, 2, 2)
F32 = jnp.float32
BF16 = jnp.bfloat16


def dot_nt(a, b):
    return lax.dot_general(a, b, (((1,), (1,)), ((), ())), preferred_element_type=F32)


def dot_nn(a, b):
    return lax.dot_general(a, b, (((1,), (0,)), ((), ())), preferred_element_type=F32)


def dot_tn(a, b):
    return lax.dot_general(a, b, (((0,), (0,)), ((), ())), preferred_element_type=F32)


def kernel(
    geometry,
    tokens_hbm,
    frozen_hbm,
    upstream_hbm,
    down_ref,
    up_ref,
    query_gain_ref,
    key_gain_ref,
    mask_ref,
    grad_hbm,
    lora_down_ref,
    lora_up_ref,
    tokens_ref,
    frozen_ref,
    load_sem,
    query_all,
    upstream_all,
    key_own,
    value_own,
    raw_ref,
    exp_all,
    product_all,
    part_out,
    part_in,
    part_own,
    stat_out,
    stat_in,
    dq_out,
    dq_in,
    dq_own,
    grad_ref,
    term_up,
    low_grad,
    bulk_send,
    bulk_recv,
    stat_send,
    stat_recv,
    dq_send,
    dq_recv,
    store_sem,
    *reduce_refs,
):
    rows, width, head_dim, dp, seq, fused = geometry
    scale = head_dim ** (-0.5)
    heads = width // head_dim
    me = lax.axis_index("seq")
    has_below = me > 0
    has_above = me < seq - 1
    edges = (has_above, has_below)
    sources = (has_below, has_above)
    targets = ({"seq": me + 1}, {"seq": me - 1})
    mesh_id = pl.DeviceIdType.MESH
    barrier = pltpu.get_barrier_semaphore()
    if fused:
        dp_me = lax.axis_index("dp")
        for j in range(1, dp):
            pl.semaphore_signal(
                barrier, inc=1, device_id={"dp": lax.rem(dp_me + j, dp)}, device_id_type=mesh_id
            )
        for j in range(1, seq):
            pl.semaphore_signal(
                barrier, inc=1, device_id={"seq": lax.rem(me + j, seq)}, device_id_type=mesh_id
            )
    else:
        for way in (0, 1):

            @pl.when(edges[way])
            def _():
                pl.semaphore_signal(
                    barrier, inc=1, device_id=targets[way], device_id_type=mesh_id
                )

    load_tokens = pltpu.make_async_copy(tokens_hbm, tokens_ref, load_sem.at[0])
    load_frozen = pltpu.make_async_copy(frozen_hbm, frozen_ref, load_sem.at[1])
    load_upstream = pltpu.make_async_copy(upstream_hbm, upstream_all.at[1], load_sem.at[2])
    load_tokens.start()
    load_frozen.start()
    load_upstream.start()

    for side in (0, 1):

        @pl.when(jnp.logical_not(sources[side]))
        def _():
            query_all[2 * side] = jnp.zeros((rows, width), BF16)
            upstream_all[2 * side] = jnp.zeros((rows, width), BF16)
            part_in[side] = jnp.zeros(part_in.shape[1:], F32)
            stat_in[side] = jnp.zeros(stat_in.shape[1:], F32)
            dq_in[side] = jnp.zeros((rows, width), BF16)

    part_out[...] = jnp.zeros(part_out.shape, F32)
    part_own[...] = jnp.zeros(part_own.shape, F32)
    stat_out[...] = jnp.zeros(stat_out.shape, F32)

    bounds = []
    first = 0
    for count in CHUNKS:
        bounds.append((first, count))
        first += count
    steps = len(bounds)

    def columns(c):
        return pl.ds(bounds[c][0] * head_dim, bounds[c][1] * head_dim)

    def remote(source, target, send, recv, way):
        return pltpu.make_async_remote_copy(
            src_ref=source,
            dst_ref=target,
            send_sem=send,
            recv_sem=recv,
            device_id=targets[way],
            device_id_type=mesh_id,
        )

    def query_copy(c, way):
        return remote(
            query_all.at[1, :, columns(c)],
            query_all.at[2 * way, :, columns(c)],
            bulk_send.at[0, way, c],
            bulk_recv.at[0, way, c],
            way,
        )

    def upstream_copy(c, way):
        return remote(
            upstream_hbm.at[:, columns(c)],
            upstream_all.at[2 * way, :, columns(c)],
            bulk_send.at[1, way, c],
            bulk_recv.at[1, way, c],
            way,
        )

    def part_copy(c, way):
        return remote(
            part_out.at[way, c],
            part_in.at[way, c],
            stat_send.at[0, way, c],
            stat_recv.at[0, way, c],
            way,
        )

    def stat_copy(c, way):
        return remote(
            stat_out.at[c],
            stat_in.at[way, c],
            stat_send.at[1, way, c],
            stat_recv.at[1, way, c],
            way,
        )

    def dq_copy(c, way):
        return remote(
            dq_out.at[way, :, columns(c)],
            dq_in.at[way, :, columns(c)],
            dq_send.at[way, c],
            dq_recv.at[way, c],
            way,
        )

    def launch(copies, c):
        for way in (0, 1):

            @pl.when(edges[way])
            def _():
                for copy in copies:
                    copy(c, way).start()

    def arrive(copies, c):
        for way in (0, 1):

            @pl.when(sources[way])
            def _():
                for copy in copies:
                    copy(c, way).wait_recv()

    def sent(copies, c):
        for way in (0, 1):

            @pl.when(edges[way])
            def _():
                for copy in copies:
                    copy(c, way).wait_send()

    if fused:
        pl.semaphore_wait(barrier, dp + seq - 2)
    else:
        for side in (0, 1):

            @pl.when(sources[side])
            def _():
                pl.semaphore_wait(barrier, 1)

    launch((upstream_copy,), 0)
    launch((upstream_copy,), 1)

    load_tokens.wait()
    low = dot_nt(tokens_ref[...], down_ref[...]).astype(BF16)
    low_t = dot_nt(down_ref[...], tokens_ref[...]).astype(BF16)
    load_frozen.wait()
    query_gain = query_gain_ref[...]
    key_gain = key_gain_ref[...]

    def normed(raw):
        inverse = lax.rsqrt(jnp.mean(raw * raw, axis=-1, keepdims=True) + EPSILON)
        return raw * inverse, inverse

    def project(part, c):
        cut = pl.ds(part * width + bounds[c][0] * head_dim, bounds[c][1] * head_dim)
        return frozen_ref[:, cut].astype(F32) + dot_nn(low, up_ref[:, cut])

    def project_heads(part, c, gain, target):
        raw = project(part, c)
        raw_ref[part, :, columns(c)] = raw
        for i in range(bounds[c][1]):
            h = bounds[c][0] + i
            one = raw[:, i * head_dim : (i + 1) * head_dim]
            target(h, (normed(one)[0] * gain).astype(BF16))

    def put_query(h, value):
        query_all[1, :, pl.ds(h * head_dim, head_dim)] = value

    def put_key(h, value):
        key_own[:, pl.ds(h * head_dim, head_dim)] = value

    for c in range(steps):
        project_heads(0, c, query_gain, put_query)
        if c == 1:
            launch((query_copy,), 0)
            launch((query_copy,), 1)
    for c in range(steps):
        project_heads(1, c, key_gain, put_key)
        value_own[:, columns(c)] = project(2, c).astype(BF16)
    load_upstream.wait()

    slot_tiles = rows

    def spread(below, own, above):
        return jnp.concatenate([below, own, above], axis=1)

    def head_cut(h):
        return pl.ds(h * head_dim, head_dim)

    def stage_scores(c):
        head, count = bounds[c]
        for i in range(count):
            h = head + i
            queries = query_all[:, :, head_cut(h)].reshape(3 * rows, head_dim)
            upstream = upstream_all[:, :, head_cut(h)].reshape(3 * rows, head_dim)
            keep_below = mask_ref[jnp.maximum(me - 1, 0), h, 1].astype(F32)
            keep_above = mask_ref[jnp.minimum(me + 1, seq - 1), h, 0].astype(F32)
            keep_below = keep_below * has_below.astype(F32)
            keep_above = keep_above * has_above.astype(F32)
            keep = spread(
                jnp.full((1, rows), keep_below, F32),
                jnp.ones((1, rows), F32),
                jnp.full((1, rows), keep_above, F32),
            )
            scores = dot_nt(key_own[:, head_cut(h)], queries) * scale
            grown = jnp.exp(scores) * keep
            product = dot_nt(value_own[:, head_cut(h)], upstream)
            exp_all[h] = grown
            product_all[h] = product
            total = jnp.sum(grown, axis=0, keepdims=True)
            moment = jnp.sum(grown * product, axis=0, keepdims=True)
            for row, line in ((i, total), (4 + i, moment)):
                part_out[1, c, pl.ds(row, 1), :] = line[:, :rows]
                part_own[c, pl.ds(row, 1), :] = line[:, rows : 2 * rows]
                part_out[0, c, pl.ds(row, 1), :] = line[:, 2 * rows :]

    def stage_stats(c):
        whole = part_own[c] + part_in[0, c] + part_in[1, c]
        count = bounds[c][1]
        inverse = 1.0 / whole[:count]
        delta = whole[4 : 4 + count] * inverse
        stat_out[c, pl.ds(0, count), :] = inverse
        stat_out[c, pl.ds(4, count), :] = delta

    def norm_grad(raw, gain, upstream):
        unit, inverse = normed(raw)
        scaled = upstream * gain
        return inverse * (scaled - unit * jnp.mean(scaled * unit, axis=-1, keepdims=True))

    def absorb(part, c):
        cut = pl.ds(part * width + bounds[c][0] * head_dim, bounds[c][1] * head_dim)
        grad = grad_ref[:, cut]
        term_up[:, cut] = dot_nn(low_t, grad)
        return dot_nt(up_ref[:, cut], grad)

    def stage_grads(c):
        head, count = bounds[c]
        for i in range(count):
            h = head + i
            queries = query_all[:, :, head_cut(h)].reshape(3 * rows, head_dim)
            upstream = upstream_all[:, :, head_cut(h)].reshape(3 * rows, head_dim)
            inverse = spread(*(ref[c, pl.ds(i, 1), :] for ref in (stat_in.at[0], stat_out, stat_in.at[1])))
            delta = spread(*(ref[c, pl.ds(4 + i, 1), :] for ref in (stat_in.at[0], stat_out, stat_in.at[1])))
            weights = exp_all[h] * inverse
            grad_scores = (weights * (product_all[h] - delta)).astype(BF16)
            grad_query = dot_tn(grad_scores, key_own[:, head_cut(h)]) * scale
            dq_out[1, :, head_cut(h)] = grad_query[:rows].astype(BF16)
            dq_own[:, head_cut(h)] = grad_query[rows : 2 * rows]
            dq_out[0, :, head_cut(h)] = grad_query[2 * rows :].astype(BF16)
        launch((dq_copy,), c)
        for i in range(count):
            h = head + i
            queries = query_all[:, :, head_cut(h)].reshape(3 * rows, head_dim)
            upstream = upstream_all[:, :, head_cut(h)].reshape(3 * rows, head_dim)
            inverse = spread(*(ref[c, pl.ds(i, 1), :] for ref in (stat_in.at[0], stat_out, stat_in.at[1])))
            delta = spread(*(ref[c, pl.ds(4 + i, 1), :] for ref in (stat_in.at[0], stat_out, stat_in.at[1])))
            weights = exp_all[h] * inverse
            grad_scores = (weights * (product_all[h] - delta)).astype(BF16)
            grad_key = dot_nn(grad_scores, queries) * scale
            grad_value = dot_nn(weights.astype(BF16), upstream)
            grad_ref[:, pl.ds(width + h * head_dim, head_dim)] = norm_grad(
                raw_ref[1, :, head_cut(h)], key_gain, grad_key
            ).astype(BF16)
            grad_ref[:, pl.ds(2 * width + h * head_dim, head_dim)] = grad_value.astype(BF16)
        low_grad[...] += absorb(1, c) + absorb(2, c)

    def stage_queries(c):
        head, count = bounds[c]
        for i in range(count):
            h = head + i
            grad_query = (
                dq_own[:, head_cut(h)]
                + dq_in[0, :, head_cut(h)].astype(F32)
                + dq_in[1, :, head_cut(h)].astype(F32)
            )
            grad_ref[:, head_cut(h)] = norm_grad(
                raw_ref[0, :, head_cut(h)], query_gain, grad_query
            ).astype(BF16)
        low_grad[...] += absorb(0, c)

    low_grad[...] = jnp.zeros(low_grad.shape, F32)
    for step in range(steps + 3):
        if step < steps:
            arrive((upstream_copy, query_copy), step)
            stage_scores(step)
            launch((part_copy,), step)
        if 0 <= step - 1 < steps:
            arrive((part_copy,), step - 1)
            stage_stats(step - 1)
            launch((stat_copy,), step - 1)
        if step + 2 < steps:
            launch((upstream_copy, query_copy), step + 2)
        if 0 <= step - 2 < steps:
            arrive((stat_copy,), step - 2)
            stage_grads(step - 2)
        if 0 <= step - 3 < steps:
            arrive((dq_copy,), step - 3)
            stage_queries(step - 3)

    store = pltpu.make_async_copy(grad_ref, grad_hbm, store_sem)
    store.start()
    model_width = tokens_ref.shape[1]
    term_down = dot_nn(low_grad[...].astype(BF16), tokens_ref[...])
    norm_factor = float(dp * seq * rows) ** (-0.5)
    if not fused:
        lora_down_ref[...] = term_down
        lora_up_ref[...] = term_up[...]
    else:
        msg_own, msg_out, msg_in, line_out, line_in, dp_send, dp_recv, seq_send, seq_recv = reduce_refs
        down_share = model_width // dp
        up_share = 3 * width // dp
        packed = msg_own.shape[2]
        filler = 2 * packed - down_share - up_share
        for d in range(dp):
            pieces = [
                term_down[:, d * down_share : (d + 1) * down_share],
                term_up[:, d * up_share : (d + 1) * up_share],
            ]
            if filler:
                pieces.append(jnp.zeros((pieces[0].shape[0], filler), F32))
            line = jnp.concatenate(pieces, axis=1)
            line = jnp.concatenate([line[:, :packed], line[:, packed:]], axis=0)
            msg_own[d] = line
            msg_out[d] = line.astype(BF16)

        def dp_copy(j):
            peer = lax.rem(dp_me + j, dp)
            return pltpu.make_async_remote_copy(
                src_ref=msg_out.at[peer],
                dst_ref=msg_in.at[j - 1],
                send_sem=dp_send.at[j - 1],
                recv_sem=dp_recv.at[j - 1],
                device_id={"dp": peer},
                device_id_type=mesh_id,
            )

        def seq_copy(j):
            peer = lax.rem(me + j, seq)
            return pltpu.make_async_remote_copy(
                src_ref=line_out,
                dst_ref=line_in.at[me],
                send_sem=seq_send.at[j - 1],
                recv_sem=seq_recv.at[j - 1],
                device_id={"seq": peer},
                device_id_type=mesh_id,
            )

        for j in range(1, dp):
            dp_copy(j).start()
        for c in range(steps):
            sent((upstream_copy, query_copy, part_copy, stat_copy, dq_copy), c)
        summed = msg_own[dp_me]
        for j in range(1, dp):
            dp_copy(j).wait_recv()
            summed = summed + msg_in[j - 1].astype(F32)
        line_out[...] = summed.astype(BF16)
        line_in[me] = summed.astype(BF16)
        for j in range(1, seq):
            seq_copy(j).start()
        for j in range(1, dp):
            dp_copy(j).wait_send()
        for j in range(1, seq):
            seq_copy(j).wait_recv()
        result = line_in[0].astype(F32)
        for j in range(1, seq):
            result = result + line_in[j].astype(F32)
        result = result * norm_factor
        half = result.shape[0] // 2
        line = jnp.concatenate([result[:half], result[half:]], axis=1)
        lora_down_ref[...] = line[:, :down_share]
        lora_up_ref[...] = line[:, down_share : down_share + up_share]
        for j in range(1, seq):
            seq_copy(j).wait_send()
    if not fused:
        for c in range(steps):
            sent((upstream_copy, query_copy, part_copy, stat_copy, dq_copy), c)
    store.wait()


def on_device(
    dp,
    seq,
    tokens,
    frozen_projection,
    output_gradient,
    adapter_down,
    adapter_up,
    query_norm_gain,
    key_norm_gain,
    neighbour_mask,
):
    clip_count, frames_dev, spatial, model_width = tokens.shape
    combined = frozen_projection.shape[-1]
    width = combined // 3
    head_dim = query_norm_gain.shape[0]
    heads = width // head_dim
    rank = adapter_up.shape[0]
    rows = clip_count * frames_dev * spatial
    assert clip_count == 1 and sum(CHUNKS) == heads
    steps = len(CHUNKS)
    down_share = model_width // dp
    up_share = combined // dp
    fused = dp <= 8 and seq <= 4 and down_share % 128 == 0
    vmem = pl.BlockSpec(memory_space=pltpu.VMEM)
    anywhere = pl.BlockSpec(memory_space=pl.ANY)
    dma = pltpu.SemaphoreType.DMA
    scratch = [
        pltpu.VMEM((rows, model_width), BF16),
        pltpu.VMEM((rows, combined), BF16),
        dma((3,)),
        pltpu.VMEM((3, rows, width), BF16),
        pltpu.VMEM((3, rows, width), BF16),
        pltpu.VMEM((rows, width), BF16),
        pltpu.VMEM((rows, width), BF16),
        pltpu.VMEM((2, rows, width), F32),
        pltpu.VMEM((heads, rows, 3 * rows), F32),
        pltpu.VMEM((heads, rows, 3 * rows), F32),
        pltpu.VMEM((2, steps, 8, rows), F32),
        pltpu.VMEM((2, steps, 8, rows), F32),
        pltpu.VMEM((steps, 8, rows), F32),
        pltpu.VMEM((steps, 8, rows), F32),
        pltpu.VMEM((2, steps, 8, rows), F32),
        pltpu.VMEM((2, rows, width), BF16),
        pltpu.VMEM((2, rows, width), BF16),
        pltpu.VMEM((rows, width), F32),
        pltpu.VMEM((rows, combined), BF16),
        pltpu.VMEM((rank, combined), F32),
        pltpu.VMEM((rank, rows), F32),
        dma((2, 2, steps)),
        dma((2, 2, steps)),
        dma((2, 2, steps)),
        dma((2, 2, steps)),
        dma((2, steps)),
        dma((2, steps)),
        dma,
    ]
    if fused:
        packed = -(-(down_share + up_share) // 256) * 128
        scratch += [
            pltpu.VMEM((dp, 2 * rank, packed), F32),
            pltpu.VMEM((dp, 2 * rank, packed), BF16),
            pltpu.VMEM((dp - 1, 2 * rank, packed), BF16),
            pltpu.VMEM((2 * rank, packed), BF16),
            pltpu.VMEM((seq, 2 * rank, packed), BF16),
            dma((dp - 1,)),
            dma((dp - 1,)),
            dma((seq - 1,)),
            dma((seq - 1,)),
        ]
        lora_shapes = ((rank, down_share), (rank, up_share))
    else:
        lora_shapes = ((rank, model_width), (rank, combined))
    geometry = (rows, width, head_dim, dp, seq, fused)
    grad, lora_down, lora_up = pl.pallas_call(
        functools.partial(kernel, geometry),
        out_shape=(
            jax.ShapeDtypeStruct((rows, combined), BF16),
            jax.ShapeDtypeStruct(lora_shapes[0], F32),
            jax.ShapeDtypeStruct(lora_shapes[1], F32),
        ),
        in_specs=[anywhere] * 3 + [vmem] * 4 + [pl.BlockSpec(memory_space=pltpu.SMEM)],
        out_specs=(anywhere, vmem, vmem),
        scratch_shapes=scratch,
        compiler_params=pltpu.CompilerParams(
            collective_id=0, has_side_effects=True, vmem_limit_bytes=48 * 1024 * 1024
        ),
        name="tile_attention",
    )(
        tokens.reshape(rows, model_width),
        frozen_projection.reshape(rows, combined),
        output_gradient.reshape(rows, width),
        adapter_down.T,
        adapter_up,
        query_norm_gain.reshape(1, head_dim),
        key_norm_gain.reshape(1, head_dim),
        neighbour_mask,
    )
    grad = grad.reshape(frozen_projection.shape)
    if fused:
        return grad, lora_down.T, lora_up
    norm_factor = float(dp * seq * rows) ** (-0.5)
    whole_down, whole_up = lax.psum((lora_down, lora_up), ("dp", "seq"))
    dp_index = lax.axis_index("dp")
    mine_down = lax.dynamic_slice_in_dim(whole_down, dp_index * down_share, down_share, 1)
    mine_up = lax.dynamic_slice_in_dim(whole_up, dp_index * up_share, up_share, 1)
    return grad, mine_down.T * norm_factor, mine_up * norm_factor


def solution(mesh):
    dp, seq = mesh.shape["dp"], mesh.shape["seq"]
    return jax.shard_map(
        functools.partial(on_device, dp, seq),
        mesh=mesh,
        in_specs=(
            P("dp", "seq", None, None),
            P("dp", "seq", None, None),
            P("dp", "seq", None, None),
            P(),
            P(),
            P(),
            P(),
            P(),
        ),
        out_specs=(P("dp", "seq", None, None), P("dp", None), P(None, "dp")),
        check_vma=False,
    )
```

time: 265 us -> 59.1 us (0.22)
  waiting for transfers between devices: 126 us -> 0 us
  local copies, waits for them, and re-layouts: 60.8 us -> 9.4 us
  Pallas kernels: 0 us -> 48.7 us
  other arithmetic: 30.9 us -> 0 us
  matrix products: 17.4 us -> 0 us
  starting transfers between devices: 13.9 us -> 0 us
  between operations: 14.3 us -> 0.65 us
    psum x1 -> x0, waiting for transfers between devices: 121 us -> none  [on_device(): whole_down, whole_up = lax.psum((term_down, term_up), ('dp', 'seq'))]
    pallas_call x0 -> x1, Pallas kernels: none -> 48.7 us  [on_device(): pl.pallas_call(functools.partial(kernel, geometry), out_shape=(jax.ShapeD...]
    dot_general x9 -> x0, matrix products: 17.4 us -> none  [the longest x1 2.99 us: attend(): jnp.einsum('hqk,hkd->hqd', grad_scores, key_bank, preferred_element_type=...]
    reshape x8 -> x0, local copies, waits for them, and re-layouts: 17.1 us -> none  [the longest x2 4.82 us: from_heads(): heads.transpose(0, 2, 1, 3)]
    ppermute x4 -> x0, starting transfers between devices: 13.8 us -> none  [shifted(): return lax.ppermute(x, axis, pairs)]
    slice x7 -> x0, local copies, waits for them, and re-layouts: 11.9 us -> none  [the longest x2 4.02 us: on_device(): value_bank = to_heads(bank[..., embed_width:], head_count)]
    mul x10 -> x0, local copies, waits for them, and re-layouts: 11.1 us -> none  [the longest x4 4.91 us: head_norm_grad(): values * inverse * inverse * inverse]
    concatenate x5 -> x0, other arithmetic: 9.72 us -> none  [the longest x2 4.39 us: on_device(): jnp.concatenate([grad_query_raw.reshape(slab_shape), grad_key_raw.reshape...]
  transfers between devices with their start and end apart: 5 -> 0, of which waited for: 3 -> 0; matrix products, arithmetic and copies ran while one was open for 16% -> 0% of each run, Pallas kernels for 0% -> 0%
where the time goes in v1:
time: 59.1 us; the launch traced here: 58.7 us
  Pallas kernels  48.7 us (82%)
  local copies, waits for them, and re-layouts  9.4 us (16%)
  between operations  0.65 us (1%)
    pallas_call x1, Pallas kernels, on_device(): pl.pallas_call(functools.partial(kernel, geometry), out_shape=(jax.ShapeD...  48.7 us
    unnamed x18, local copies, waits for them, and re-layouts  9.4 us

profile of v1, /device:TPU:0, one launch (start us, length us, event | category | flops | bytes accessed | tf_op | source)
XLA Modules:
  0.0 58.7 jit_solution(103713289178040679)
XLA Ops:
  0.6 0.8 %copy.11.mask_ref = s32[4,12,2]{2,1,0:T(8,128)S(1)} copy(s32[4,12,2]{1,2,0:T(2,128)} %param.15) | data formatting | bytes 768 | tf_op args[7]
  1.4 0.0 copy-start
  1.4 1.3 %copy-done = bf16[1,2,64,4608]{3,2,1,0:T(8,128)(2,1)S(1)} copy-done((bf16[1,2,64,4608]{3,2,1,0:T(8,128)(2,1)S(1)}, bf16[1,2,64,4608]{3,2,1,0:T(8,128)(2,1)}, u32[]{:S(2)}) %copy-start) | copy-done | bytes 1179672
  2.7 0.0 copy-start.1
  2.7 1.1 %copy-done.1 = bf16[1,2,64,3072]{3,2,1,0:T(8,128)(2,1)S(1)} copy-done((bf16[1,2,64,3072]{3,2,1,0:T(8,128)(2,1)S(1)}, bf16[1,2,64,3072]{3,2,1,0:T(8,128)(2,1)}, u32[]{:S(2)}) %copy-start.1) | copy-done | bytes 786456
  3.8 0.0 copy-start.2
  3.8 1.0 %copy-done.2 = bf16[1,2,64,1536]{3,2,1,0:T(8,128)(2,1)S(1)} copy-done((bf16[1,2,64,1536]{3,2,1,0:T(8,128)(2,1)S(1)}, bf16[1,2,64,1536]{3,2,1,0:T(8,128)(2,1)}, u32[]{:S(2)}) %copy-start.2) | copy-done | bytes 393240
  4.8 0.0 copy-start.3
  4.8 0.9 %copy-done.3 = bf16[8,4608]{1,0:T(8,128)(2,1)S(1)} copy-done((bf16[8,4608]{1,0:T(8,128)(2,1)S(1)}, bf16[8,4608]{1,0:T(8,128)(2,1)}, u32[]{:S(2)}) %copy-start.3) | copy-done | bytes 73752
  5.7 0.0 copy-start.4
  5.7 0.8 %copy-done.4 = bf16[3072,8]{0,1:T(8,128)(2,1)S(1)} copy-done((bf16[3072,8]{0,1:T(8,128)(2,1)S(1)}, bf16[3072,8]{0,1:T(8,128)(2,1)}, u32[]{:S(2)}) %copy-start.4) | copy-done | bytes 49176
  6.5 0.0 copy-start.5
  6.5 0.7 %copy-done.5 = f32[128]{0:T(128)S(1)} copy-done((f32[128]{0:T(128)S(1)}, f32[128]{0:T(128)}, u32[]{:S(2)}) %copy-start.5) | copy-done | bytes 536
  7.2 0.0 copy-start.6
  7.2 0.7 %copy-done.6 = f32[128]{0:T(128)S(1)} copy-done((f32[128]{0:T(128)S(1)}, f32[128]{0:T(128)}, u32[]{:S(2)}) %copy-start.6) | copy-done | bytes 536
  7.8 48.7 %tile_attention.1 = (bf16[128,4608]{1,0:T(8,128)(2,1)S(1)}, f32[8,384]{1,0:T(8,128)S(1)}, f32[8,576]{1,0:T(8,128)S(1)}) custom-call(bf16[128,3072]{1,0:T(8,128)(2,1)S(1)} %bitcast.10, bf16[128,4608]{1,0:T(8,128)(2,1)S(1)} %bitcast.8, bf16[128,1536]{1,0:T(8,128)(2,1)S(1)} %bitcast.11, bf16[8,3072]{1,0:T(8,128)(2,1)S(1)} %bitcast.12, ...), custom_call_target="tpu_custom_call" | custom-call | tf_op jit(solution)/shard_map/tile_attention/pallas_call | solution.py:534
  56.5 1.0 %copy.15 = bf16[1,2,64,4608]{3,2,1,0:T(8,128)(2,1)} copy(bf16[1,2,64,4608]{3,2,1,0:T(8,128)(2,1)S(1)} %bitcast.9) | data formatting | bytes 2359296
  57.5 0.6 %copy.16 = f32[384,8]{0,1:T(8,128)} copy(f32[384,8]{0,1:T(8,128)S(1)} %bitcast.13) | data formatting | bytes 24576
  58.1 0.6 %copy.17 = f32[8,576]{1,0:T(8,128)} copy(f32[8,576]{1,0:T(8,128)S(1)} %get-tuple-element.14) | data formatting | bytes 36864
Async XLA Ops:
  1.4 1.3 %copy-start = (bf16[1,2,64,4608]{3,2,1,0:T(8,128)(2,1)S(1)}, bf16[1,2,64,4608]{3,2,1,0:T(8,128)(2,1)}, u32[]{:S(2)}) copy-start(bf16[1,2,64,4608]{3,2,1,0:T(8,128)(2,1)} %param.9) | copy-start | bytes 3538948
  2.7 1.1 %copy-start.1 = (bf16[1,2,64,3072]{3,2,1,0:T(8,128)(2,1)S(1)}, bf16[1,2,64,3072]{3,2,1,0:T(8,128)(2,1)}, u32[]{:S(2)}) copy-start(bf16[1,2,64,3072]{3,2,1,0:T(8,128)(2,1)} %param.8) | copy-start | bytes 2359300
  3.8 1.0 %copy-start.2 = (bf16[1,2,64,1536]{3,2,1,0:T(8,128)(2,1)S(1)}, bf16[1,2,64,1536]{3,2,1,0:T(8,128)(2,1)}, u32[]{:S(2)}) copy-start(bf16[1,2,64,1536]{3,2,1,0:T(8,128)(2,1)} %param.10) | copy-start | bytes 1179652
  4.8 0.9 %copy-start.3 = (bf16[8,4608]{1,0:T(8,128)(2,1)S(1)}, bf16[8,4608]{1,0:T(8,128)(2,1)}, u32[]{:S(2)}) copy-start(bf16[8,4608]{1,0:T(8,128)(2,1)} %up_ref.1) | copy-start | bytes 221188
  5.7 0.8 %copy-start.4 = (bf16[3072,8]{0,1:T(8,128)(2,1)S(1)}, bf16[3072,8]{0,1:T(8,128)(2,1)}, u32[]{:S(2)}) copy-start(bf16[3072,8]{0,1:T(8,128)(2,1)} %param.11) | copy-start | bytes 147460
  6.5 0.7 %copy-start.5 = (f32[128]{0:T(128)S(1)}, f32[128]{0:T(128)}, u32[]{:S(2)}) copy-start(f32[128]{0:T(128)} %param.13) | copy-start | bytes 1540
  7.2 0.7 %copy-start.6 = (f32[128]{0:T(128)S(1)}, f32[128]{0:T(128)}, u32[]{:S(2)}) copy-start(f32[128]{0:T(128)} %param.14) | copy-start | bytes 1540

commit v2 on v1

--- a/solution.py
+++ b/solution.py
@@ -9,6 +9,7 @@
 
 EPSILON = 1e-06
 CHUNKS = (2, 2, 2, 2, 2, 2)
+LEAD = 2
 F32 = jnp.float32
 BF16 = jnp.bfloat16
 
@@ -30,16 +31,21 @@
     tokens_hbm,
     frozen_hbm,
     upstream_hbm,
+    down_hbm,
+    up_hbm,
+    query_gain_hbm,
+    key_gain_hbm,
+    mask_hbm,
+    grad_ref,
+    lora_down_ref,
+    lora_up_ref,
+    tokens_ref,
+    frozen_ref,
     down_ref,
     up_ref,
     query_gain_ref,
     key_gain_ref,
     mask_ref,
-    grad_hbm,
-    lora_down_ref,
-    lora_up_ref,
-    tokens_ref,
-    frozen_ref,
     load_sem,
     query_all,
     upstream_all,
@@ -56,7 +62,6 @@
     dq_out,
     dq_in,
     dq_own,
-    grad_ref,
     term_up,
     low_grad,
     bulk_send,
@@ -65,7 +70,6 @@
     stat_recv,
     dq_send,
     dq_recv,
-    store_sem,
     *reduce_refs,
 ):
     rows, width, head_dim, dp, seq, fused = geometry
@@ -101,7 +105,21 @@
     load_tokens = pltpu.make_async_copy(tokens_hbm, tokens_ref, load_sem.at[0])
     load_frozen = pltpu.make_async_copy(frozen_hbm, frozen_ref, load_sem.at[1])
     load_upstream = pltpu.make_async_copy(upstream_hbm, upstream_all.at[1], load_sem.at[2])
+    load_small = [
+        pltpu.make_async_copy(source, target, load_sem.at[3 + i])
+        for i, (source, target) in enumerate(
+            (
+                (down_hbm, down_ref),
+                (up_hbm, up_ref),
+                (query_gain_hbm, query_gain_ref),
+                (key_gain_hbm, key_gain_ref),
+                (mask_hbm, mask_ref),
+            )
+        )
+    ]
     load_tokens.start()
+    for load in load_small:
+        load.start()
     load_frozen.start()
     load_upstream.start()
 
@@ -217,12 +235,13 @@
             def _():
                 pl.semaphore_wait(barrier, 1)
 
-    launch((upstream_copy,), 0)
-    launch((upstream_copy,), 1)
+    for c in range(LEAD):
+        launch((upstream_copy,), c)
 
     load_tokens.wait()
+    for load in load_small:
+        load.wait()
     low = dot_nt(tokens_ref[...], down_ref[...]).astype(BF16)
-    low_t = dot_nt(down_ref[...], tokens_ref[...]).astype(BF16)
     load_frozen.wait()
     query_gain = query_gain_ref[...]
     key_gain = key_gain_ref[...]
@@ -249,17 +268,17 @@
     def put_key(h, value):
         key_own[:, pl.ds(h * head_dim, head_dim)] = value
 
-    for c in range(steps):
+    for c in range(LEAD):
         project_heads(0, c, query_gain, put_query)
-        if c == 1:
-            launch((query_copy,), 0)
-            launch((query_copy,), 1)
-    for c in range(steps):
+        launch((query_copy,), c)
+
+    def project_bank(c):
         project_heads(1, c, key_gain, put_key)
         value_own[:, columns(c)] = project(2, c).astype(BF16)
+
+    project_bank(0)
     load_upstream.wait()
-
-    slot_tiles = rows
+    low_t = dot_nt(down_ref[...], tokens_ref[...]).astype(BF16)
 
     def spread(below, own, above):
         return jnp.concatenate([below, own, above], axis=1)
@@ -273,8 +292,8 @@
             h = head + i
             queries = query_all[:, :, head_cut(h)].reshape(3 * rows, head_dim)
             upstream = upstream_all[:, :, head_cut(h)].reshape(3 * rows, head_dim)
-            keep_below = mask_ref[jnp.maximum(me - 1, 0), h, 1].astype(F32)
-            keep_above = mask_ref[jnp.minimum(me + 1, seq - 1), h, 0].astype(F32)
+            keep_below = mask_ref[jnp.maximum(me - 1, 0), 1, h].astype(F32)
+            keep_above = mask_ref[jnp.minimum(me + 1, seq - 1), 0, h].astype(F32)
             keep_below = keep_below * has_below.astype(F32)
             keep_above = keep_above * has_above.astype(F32)
             keep = spread(
@@ -315,14 +334,21 @@
 
     def stage_grads(c):
         head, count = bounds[c]
+        held = []
         for i in range(count):
             h = head + i
-            queries = query_all[:, :, head_cut(h)].reshape(3 * rows, head_dim)
-            upstream = upstream_all[:, :, head_cut(h)].reshape(3 * rows, head_dim)
-            inverse = spread(*(ref[c, pl.ds(i, 1), :] for ref in (stat_in.at[0], stat_out, stat_in.at[1])))
-            delta = spread(*(ref[c, pl.ds(4 + i, 1), :] for ref in (stat_in.at[0], stat_out, stat_in.at[1])))
+            inverse, delta = (
+                spread(
+                    *(
+                        ref[c, pl.ds(row, 1), :]
+                        for ref in (stat_in.at[0], stat_out, stat_in.at[1])
+                    )
+                )
+                for row in (i, 4 + i)
+            )
             weights = exp_all[h] * inverse
             grad_scores = (weights * (product_all[h] - delta)).astype(BF16)
+            held.append((weights.astype(BF16), grad_scores))
             grad_query = dot_tn(grad_scores, key_own[:, head_cut(h)]) * scale
             dq_out[1, :, head_cut(h)] = grad_query[:rows].astype(BF16)
             dq_own[:, head_cut(h)] = grad_query[rows : 2 * rows]
@@ -330,14 +356,11 @@
         launch((dq_copy,), c)
         for i in range(count):
             h = head + i
+            weights_low, grad_scores = held[i]
             queries = query_all[:, :, head_cut(h)].reshape(3 * rows, head_dim)
             upstream = upstream_all[:, :, head_cut(h)].reshape(3 * rows, head_dim)
-            inverse = spread(*(ref[c, pl.ds(i, 1), :] for ref in (stat_in.at[0], stat_out, stat_in.at[1])))
-            delta = spread(*(ref[c, pl.ds(4 + i, 1), :] for ref in (stat_in.at[0], stat_out, stat_in.at[1])))
-            weights = exp_all[h] * inverse
-            grad_scores = (weights * (product_all[h] - delta)).astype(BF16)
             grad_key = dot_nn(grad_scores, queries) * scale
-            grad_value = dot_nn(weights.astype(BF16), upstream)
+            grad_value = dot_nn(weights_low, upstream)
             grad_ref[:, pl.ds(width + h * head_dim, head_dim)] = norm_grad(
                 raw_ref[1, :, head_cut(h)], key_gain, grad_key
             ).astype(BF16)
@@ -364,12 +387,16 @@
             arrive((upstream_copy, query_copy), step)
             stage_scores(step)
             launch((part_copy,), step)
+        if step + LEAD < steps:
+            project_heads(0, step + LEAD, query_gain, put_query)
         if 0 <= step - 1 < steps:
             arrive((part_copy,), step - 1)
             stage_stats(step - 1)
             launch((stat_copy,), step - 1)
-        if step + 2 < steps:
-            launch((upstream_copy, query_copy), step + 2)
+        if step + LEAD < steps:
+            launch((upstream_copy, query_copy), step + LEAD)
+        if step + 1 < steps:
+            project_bank(step + 1)
         if 0 <= step - 2 < steps:
             arrive((stat_copy,), step - 2)
             stage_grads(step - 2)
@@ -377,8 +404,6 @@
             arrive((dq_copy,), step - 3)
             stage_queries(step - 3)
 
-    store = pltpu.make_async_copy(grad_ref, grad_hbm, store_sem)
-    store.start()
     model_width = tokens_ref.shape[1]
     term_down = dot_nn(low_grad[...].astype(BF16), tokens_ref[...])
     norm_factor = float(dp * seq * rows) ** (-0.5)
@@ -454,7 +479,30 @@
     if not fused:
         for c in range(steps):
             sent((upstream_copy, query_copy, part_copy, stat_copy, dq_copy), c)
-    store.wait()
+
+
+def writer(*refs):
+    sources, targets, sem = refs[:3], refs[3:6], refs[6]
+    copies = [
+        pltpu.make_async_copy(source, target, sem.at[i])
+        for i, (source, target) in enumerate(zip(sources, targets))
+    ]
+    for copy in copies:
+        copy.start()
+    for copy in copies:
+        copy.wait()
+
+
+def write_out(*arrays):
+    return pl.pallas_call(
+        writer,
+        out_shape=tuple(jax.ShapeDtypeStruct(a.shape, a.dtype) for a in arrays),
+        in_specs=[pl.BlockSpec(memory_space=pltpu.VMEM)] * 3,
+        out_specs=(pl.BlockSpec(memory_space=pltpu.HBM),) * 3,
+        scratch_shapes=[pltpu.SemaphoreType.DMA((3,))],
+        compiler_params=pltpu.CompilerParams(vmem_limit_bytes=4 * 1024 * 1024),
+        name="write_out",
+    )(*arrays)
 
 
 def on_device(
@@ -481,13 +529,19 @@
     down_share = model_width // dp
     up_share = combined // dp
     fused = dp <= 8 and seq <= 4 and down_share % 128 == 0
+    mask_shape = (neighbour_mask.shape[0], 2, heads)
     vmem = pl.BlockSpec(memory_space=pltpu.VMEM)
-    anywhere = pl.BlockSpec(memory_space=pl.ANY)
+    distant = pl.BlockSpec(memory_space=pltpu.HBM)
     dma = pltpu.SemaphoreType.DMA
     scratch = [
         pltpu.VMEM((rows, model_width), BF16),
         pltpu.VMEM((rows, combined), BF16),
-        dma((3,)),
+        pltpu.VMEM((rank, model_width), BF16),
+        pltpu.VMEM((rank, combined), BF16),
+        pltpu.VMEM((1, head_dim), F32),
+        pltpu.VMEM((1, head_dim), F32),
+        pltpu.SMEM(mask_shape, jnp.int32),
+        dma((8,)),
         pltpu.VMEM((3, rows, width), BF16),
         pltpu.VMEM((3, rows, width), BF16),
         pltpu.VMEM((rows, width), BF16),
@@ -503,7 +557,6 @@
         pltpu.VMEM((2, rows, width), BF16),
         pltpu.VMEM((2, rows, width), BF16),
         pltpu.VMEM((rows, width), F32),
-        pltpu.VMEM((rows, combined), BF16),
         pltpu.VMEM((rank, combined), F32),
         pltpu.VMEM((rank, rows), F32),
         dma((2, 2, steps)),
@@ -512,7 +565,6 @@
         dma((2, 2, steps)),
         dma((2, steps)),
         dma((2, steps)),
-        dma,
     ]
     if fused:
         packed = -(-(down_share + up_share) // 256) * 128
@@ -538,23 +590,30 @@
             jax.ShapeDtypeStruct(lora_shapes[0], F32),
             jax.ShapeDtypeStruct(lora_shapes[1], F32),
         ),
-        in_specs=[anywhere] * 3 + [vmem] * 4 + [pl.BlockSpec(memory_space=pltpu.SMEM)],
-        out_specs=(anywhere, vmem, vmem),
+        in_specs=[distant] * 8,
+        out_specs=(vmem, vmem, vmem),
         scratch_shapes=scratch,
         compiler_params=pltpu.CompilerParams(
             collective_id=0, has_side_effects=True, vmem_limit_bytes=48 * 1024 * 1024
         ),
         name="tile_attention",
     )(
-        tokens.reshape(rows, model_width),
-        frozen_projection.reshape(rows, combined),
-        output_gradient.reshape(rows, width),
-        adapter_down.T,
-        adapter_up,
-        query_norm_gain.reshape(1, head_dim),
-        key_norm_gain.reshape(1, head_dim),
-        neighbour_mask,
+        *(
+            pltpu.with_memory_space_constraint(array, pltpu.HBM)
+            for array in (
+                tokens.reshape(rows, model_width),
+                frozen_projection.reshape(rows, combined),
+                output_gradient.reshape(rows, width),
+                adapter_down.T,
+                adapter_up,
+                query_norm_gain.reshape(1, head_dim),
+                key_norm_gain.reshape(1, head_dim),
+                neighbour_mask.transpose(0, 2, 1),
+            )
+        )
     )
+    if fused:
+        grad, lora_down, lora_up = write_out(grad, lora_down, lora_up)
     grad = grad.reshape(frozen_projection.shape)
     if fused:
         return grad, lora_down.T, lora_up

time: 59.1 us -> 49.6 us (0.84)
  local copies, waits for them, and re-layouts: 9.4 us -> 0 us
    unnamed x18 -> x0, local copies, waits for them, and re-layouts: 9.4 us -> none
    pallas_call x0 -> x1, Pallas kernels: none -> 1.05 us  [write_out(): pl.pallas_call(writer, out_shape=tuple((jax.ShapeDtypeStruct(a.shape, a.d...]
    pallas_call x1, Pallas kernels: 48.7 us -> 47.8 us  [on_device(): pl.pallas_call(functools.partial(kernel, geometry), out_shape=(jax.ShapeD...]
where the time goes in v2:
time: 49.6 us; the launch traced here: 49.5 us
  Pallas kernels  48.9 us (99%)
  between operations  0.64 us (1%)
    pallas_call x1, Pallas kernels, on_device(): pl.pallas_call(functools.partial(kernel, geometry), out_shape=(jax.ShapeD...  47.8 us
    pallas_call x1, Pallas kernels, write_out(): pl.pallas_call(writer, out_shape=tuple((jax.ShapeDtypeStruct(a.shape, a.d...  1.05 us

profile of v2, /device:TPU:0, one launch (start us, length us, event | category | flops | bytes accessed | tf_op | source)
XLA Modules:
  0.0 49.5 jit_solution(13127493221973860090)
XLA Ops:
  0.6 47.8 %tile_attention.1 = (bf16[128,4608]{1,0:T(8,128)(2,1)S(1)}, f32[8,384]{1,0:T(8,128)S(1)}, f32[8,576]{1,0:T(8,128)S(1)}) custom-call(bf16[128,3072]{1,0:T(8,128)(2,1)} %bitcast.10, bf16[128,4608]{1,0:T(8,128)(2,1)} %bitcast.9, bf16[128,1536]{1,0:T(8,128)(2,1)} %bitcast.11, bf16[8,3072]{1,0:T(8,128)(2,1)} %bitcast.12, bf16[8,4608]{1,0:T(8,128)(2,1)} %up_hbm.1, ...), custom_call_target="tpu_custom_call" | custom-call | tf_op jit(solution)/shard_map/tile_attention/pallas_call | solution.py:586
  48.4 1.0 %write_out.1 = (bf16[128,4608]{1,0:T(8,128)(2,1)}, f32[8,384]{1,0:T(8,128)}, f32[8,576]{1,0:T(8,128)}) custom-call(bf16[128,4608]{1,0:T(8,128)(2,1)S(1)} %get-tuple-element.9.refs_0_, f32[8,384]{1,0:T(8,128)S(1)} %get-tuple-element.10.refs_1_, f32[8,576]{1,0:T(8,128)S(1)} %get-tuple-element.11.refs_2_), custom_call_target="tpu_custom_call" | custom-call | tf_op jit(solution)/shard_map/write_out/pallas_call | solution.py:497

commit v3 on v2

--- a/solution.py
+++ b/solution.py
@@ -8,8 +8,9 @@
 from jax.sharding import PartitionSpec as P
 
 EPSILON = 1e-06
-CHUNKS = (2, 2, 2, 2, 2, 2)
+CHUNKS = (3, 4, 3, 2)
 LEAD = 2
+LAGS = (1, 2, 3)
 F32 = jnp.float32
 BF16 = jnp.bfloat16
 
@@ -104,9 +105,14 @@
 
     load_tokens = pltpu.make_async_copy(tokens_hbm, tokens_ref, load_sem.at[0])
     load_frozen = pltpu.make_async_copy(frozen_hbm, frozen_ref, load_sem.at[1])
-    load_upstream = pltpu.make_async_copy(upstream_hbm, upstream_all.at[1], load_sem.at[2])
+    load_upstream = [
+        pltpu.make_async_copy(
+            upstream_hbm.at[:, pl.ds(h * head_dim, head_dim)], upstream_all.at[1, h], load_sem.at[7 + h]
+        )
+        for h in range(heads)
+    ]
     load_small = [
-        pltpu.make_async_copy(source, target, load_sem.at[3 + i])
+        pltpu.make_async_copy(source, target, load_sem.at[2 + i])
         for i, (source, target) in enumerate(
             (
                 (down_hbm, down_ref),
@@ -117,21 +123,22 @@
             )
         )
     ]
+    for load in load_upstream:
+        load.start()
     load_tokens.start()
     for load in load_small:
         load.start()
     load_frozen.start()
-    load_upstream.start()
 
     for side in (0, 1):
 
         @pl.when(jnp.logical_not(sources[side]))
         def _():
-            query_all[2 * side] = jnp.zeros((rows, width), BF16)
-            upstream_all[2 * side] = jnp.zeros((rows, width), BF16)
+            query_all[2 * side] = jnp.zeros((heads, rows, head_dim), BF16)
+            upstream_all[2 * side] = jnp.zeros((heads, rows, head_dim), BF16)
             part_in[side] = jnp.zeros(part_in.shape[1:], F32)
             stat_in[side] = jnp.zeros(stat_in.shape[1:], F32)
-            dq_in[side] = jnp.zeros((rows, width), BF16)
+            dq_in[side] = jnp.zeros((heads, rows, head_dim), BF16)
 
     part_out[...] = jnp.zeros(part_out.shape, F32)
     part_own[...] = jnp.zeros(part_own.shape, F32)
@@ -146,6 +153,9 @@
 
     def columns(c):
         return pl.ds(bounds[c][0] * head_dim, bounds[c][1] * head_dim)
+
+    def members(c):
+        return pl.ds(*bounds[c])
 
     def remote(source, target, send, recv, way):
         return pltpu.make_async_remote_copy(
@@ -159,8 +169,8 @@
 
     def query_copy(c, way):
         return remote(
-            query_all.at[1, :, columns(c)],
-            query_all.at[2 * way, :, columns(c)],
+            query_all.at[1, members(c)],
+            query_all.at[2 * way, members(c)],
             bulk_send.at[0, way, c],
             bulk_recv.at[0, way, c],
             way,
@@ -168,8 +178,8 @@
 
     def upstream_copy(c, way):
         return remote(
-            upstream_hbm.at[:, columns(c)],
-            upstream_all.at[2 * way, :, columns(c)],
+            upstream_all.at[1, members(c)],
+            upstream_all.at[2 * way, members(c)],
             bulk_send.at[1, way, c],
             bulk_recv.at[1, way, c],
             way,
@@ -195,8 +205,8 @@
 
     def dq_copy(c, way):
         return remote(
-            dq_out.at[way, :, columns(c)],
-            dq_in.at[way, :, columns(c)],
+            dq_out.at[way, members(c)],
+            dq_in.at[way, members(c)],
             dq_send.at[way, c],
             dq_recv.at[way, c],
             way,
@@ -235,8 +245,9 @@
             def _():
                 pl.semaphore_wait(barrier, 1)
 
-    for c in range(LEAD):
-        launch((upstream_copy,), c)
+    for load in load_upstream:
+        load.wait()
+    launch((upstream_copy,), 0)
 
     load_tokens.wait()
     for load in load_small:
@@ -263,7 +274,7 @@
             target(h, (normed(one)[0] * gain).astype(BF16))
 
     def put_query(h, value):
-        query_all[1, :, pl.ds(h * head_dim, head_dim)] = value
+        query_all[1, h] = value
 
     def put_key(h, value):
         key_own[:, pl.ds(h * head_dim, head_dim)] = value
@@ -271,13 +282,14 @@
     for c in range(LEAD):
         project_heads(0, c, query_gain, put_query)
         launch((query_copy,), c)
+        if c + 1 < LEAD:
+            launch((upstream_copy,), c + 1)
 
     def project_bank(c):
         project_heads(1, c, key_gain, put_key)
         value_own[:, columns(c)] = project(2, c).astype(BF16)
 
     project_bank(0)
-    load_upstream.wait()
     low_t = dot_nt(down_ref[...], tokens_ref[...]).astype(BF16)
 
     def spread(below, own, above):
@@ -290,8 +302,8 @@
         head, count = bounds[c]
         for i in range(count):
             h = head + i
-            queries = query_all[:, :, head_cut(h)].reshape(3 * rows, head_dim)
-            upstream = upstream_all[:, :, head_cut(h)].reshape(3 * rows, head_dim)
+            queries = query_all[:, h].reshape(3 * rows, head_dim)
+            upstream = upstream_all[:, h].reshape(3 * rows, head_dim)
             keep_below = mask_ref[jnp.maximum(me - 1, 0), 1, h].astype(F32)
             keep_above = mask_ref[jnp.minimum(me + 1, seq - 1), 0, h].astype(F32)
             keep_below = keep_below * has_below.astype(F32)
@@ -350,15 +362,15 @@
             grad_scores = (weights * (product_all[h] - delta)).astype(BF16)
             held.append((weights.astype(BF16), grad_scores))
             grad_query = dot_tn(grad_scores, key_own[:, head_cut(h)]) * scale
-            dq_out[1, :, head_cut(h)] = grad_query[:rows].astype(BF16)
+            dq_out[1, h] = grad_query[:rows].astype(BF16)
             dq_own[:, head_cut(h)] = grad_query[rows : 2 * rows]
-            dq_out[0, :, head_cut(h)] = grad_query[2 * rows :].astype(BF16)
+            dq_out[0, h] = grad_query[2 * rows :].astype(BF16)
         launch((dq_copy,), c)
         for i in range(count):
             h = head + i
             weights_low, grad_scores = held[i]
-            queries = query_all[:, :, head_cut(h)].reshape(3 * rows, head_dim)
-            upstream = upstream_all[:, :, head_cut(h)].reshape(3 * rows, head_dim)
+            queries = query_all[:, h].reshape(3 * rows, head_dim)
+            upstream = upstream_all[:, h].reshape(3 * rows, head_dim)
             grad_key = dot_nn(grad_scores, queries) * scale
             grad_value = dot_nn(weights_low, upstream)
             grad_ref[:, pl.ds(width + h * head_dim, head_dim)] = norm_grad(
@@ -373,8 +385,8 @@
             h = head + i
             grad_query = (
                 dq_own[:, head_cut(h)]
-                + dq_in[0, :, head_cut(h)].astype(F32)
-                + dq_in[1, :, head_cut(h)].astype(F32)
+                + dq_in[0, h].astype(F32)
+                + dq_in[1, h].astype(F32)
             )
             grad_ref[:, head_cut(h)] = norm_grad(
                 raw_ref[0, :, head_cut(h)], query_gain, grad_query
@@ -382,27 +394,30 @@
         low_grad[...] += absorb(0, c)
 
     low_grad[...] = jnp.zeros(low_grad.shape, F32)
-    for step in range(steps + 3):
+    for step in range(steps + LAGS[2]):
         if step < steps:
             arrive((upstream_copy, query_copy), step)
             stage_scores(step)
             launch((part_copy,), step)
         if step + LEAD < steps:
             project_heads(0, step + LEAD, query_gain, put_query)
-        if 0 <= step - 1 < steps:
-            arrive((part_copy,), step - 1)
-            stage_stats(step - 1)
-            launch((stat_copy,), step - 1)
+        past = step - LAGS[0]
+        if 0 <= past < steps:
+            arrive((part_copy,), past)
+            stage_stats(past)
+            launch((stat_copy,), past)
         if step + LEAD < steps:
             launch((upstream_copy, query_copy), step + LEAD)
         if step + 1 < steps:
             project_bank(step + 1)
-        if 0 <= step - 2 < steps:
-            arrive((stat_copy,), step - 2)
-            stage_grads(step - 2)
-        if 0 <= step - 3 < steps:
-            arrive((dq_copy,), step - 3)
-            stage_queries(step - 3)
+        past = step - LAGS[1]
+        if 0 <= past < steps:
+            arrive((stat_copy,), past)
+            stage_grads(past)
+        past = step - LAGS[2]
+        if 0 <= past < steps:
+            arrive((dq_copy,), past)
+            stage_queries(past)
 
     model_width = tokens_ref.shape[1]
     term_down = dot_nn(low_grad[...].astype(BF16), tokens_ref[...])
@@ -541,9 +556,9 @@
         pltpu.VMEM((1, head_dim), F32),
         pltpu.VMEM((1, head_dim), F32),
         pltpu.SMEM(mask_shape, jnp.int32),
-        dma((8,)),
-        pltpu.VMEM((3, rows, width), BF16),
-        pltpu.VMEM((3, rows, width), BF16),
+        dma((7 + heads,)),
+        pltpu.VMEM((3, heads, rows, head_dim), BF16),
+        pltpu.VMEM((3, heads, rows, head_dim), BF16),
         pltpu.VMEM((rows, width), BF16),
         pltpu.VMEM((rows, width), BF16),
         pltpu.VMEM((2, rows, width), F32),
@@ -554,8 +569,8 @@
         pltpu.VMEM((steps, 8, rows), F32),
         pltpu.VMEM((steps, 8, rows), F32),
         pltpu.VMEM((2, steps, 8, rows), F32),
-        pltpu.VMEM((2, rows, width), BF16),
-        pltpu.VMEM((2, rows, width), BF16),
+        pltpu.VMEM((2, heads, rows, head_dim), BF16),
+        pltpu.VMEM((2, heads, rows, head_dim), BF16),
         pltpu.VMEM((rows, width), F32),
         pltpu.VMEM((rank, combined), F32),
         pltpu.VMEM((rank, rows), F32),

time: 49.6 us -> 45.8 us (0.923)
  Pallas kernels: 48.9 us -> 45 us
    pallas_call x1, Pallas kernels: 47.8 us -> 43.9 us  [on_device(): pl.pallas_call(functools.partial(kernel, geometry), out_shape=(jax.ShapeD...]
where the time goes in v3:
time: 45.8 us; the launch traced here: 45.6 us
  Pallas kernels  45 us (98%)
  between operations  0.64 us (1%)
    pallas_call x1, Pallas kernels, on_device(): pl.pallas_call(functools.partial(kernel, geometry), out_shape=(jax.ShapeD...  43.9 us
    pallas_call x1, Pallas kernels, write_out(): pl.pallas_call(writer, out_shape=tuple((jax.ShapeDtypeStruct(a.shape, a.d...  1.05 us

profile of v3, /device:TPU:0, one launch (start us, length us, event | category | flops | bytes accessed | tf_op | source)
XLA Modules:
  0.0 45.6 jit_solution(12540830087999346284)
XLA Ops:
  0.6 43.9 %tile_attention.1 = (bf16[128,4608]{1,0:T(8,128)(2,1)S(1)}, f32[8,384]{1,0:T(8,128)S(1)}, f32[8,576]{1,0:T(8,128)S(1)}) custom-call(bf16[128,3072]{1,0:T(8,128)(2,1)} %bitcast.10, bf16[128,4608]{1,0:T(8,128)(2,1)} %bitcast.9, bf16[128,1536]{1,0:T(8,128)(2,1)} %bitcast.11, bf16[8,3072]{1,0:T(8,128)(2,1)} %bitcast.12, bf16[8,4608]{1,0:T(8,128)(2,1)} %up_hbm.1, ...), custom_call_target="tpu_custom_call" | custom-call | tf_op jit(solution)/shard_map/tile_attention/pallas_call | solution.py:601
  44.6 1.0 %write_out.1 = (bf16[128,4608]{1,0:T(8,128)(2,1)}, f32[8,384]{1,0:T(8,128)}, f32[8,576]{1,0:T(8,128)}) custom-call(bf16[128,4608]{1,0:T(8,128)(2,1)S(1)} %get-tuple-element.9.refs_0_, f32[8,384]{1,0:T(8,128)S(1)} %get-tuple-element.10.refs_1_, f32[8,576]{1,0:T(8,128)S(1)} %get-tuple-element.11.refs_2_), custom_call_target="tpu_custom_call" | custom-call | tf_op jit(solution)/shard_map/write_out/pallas_call | solution.py:512
